TPU v7x, 32 devices: a whole 2x2x4 slice. The times are simulated.
32 devices in a mesh: leaf: 32 (over z, y, x, core).
Axes of the slice: x: 2, y: 2, z: 4, core: 2. Of those that a mesh axis runs over, the one named last changes fastest.
Arguments:
- points: bfloat16 [64, 32768], P(None, 'leaf'), may hold values from -6 to 6
- weights: bfloat16 [32768, 512], P('leaf'), may hold values from -1.1953125 to 1.1953125
- interp: bfloat16 [32768, 512], P('leaf'), may hold values from -0.1875 to 0.1875
- transfers: bfloat16 [32, 5, 512, 512], P('leaf'), may hold values from -0.25 to 0.25
- near_mask: int32 [32, 4], P('leaf'), may hold values 0 or 1
- skel_index: int32 [32, 512], P('leaf'), may hold values from 0 to 1023, as said below
Outputs:
- product: bfloat16 [32768, 512], P('leaf')
Inputs may be any that keep to these rules, and one draw needn't show every extreme that they name: `skel_index`: each row holds 512 distinct ranks.
All inputs are finite; a program needn't handle non-finite values. No bound on the sum of `near_mask` on one device may be relied on, other than what follows from the above.
Results may differ from a plain program's by a relative error of at most 0.0075.
Values may be sent and summed in bfloat16 or wider, within the bound.
A program may use at most 128 MiB of HBM per device.

v0:
```python
import functools
import math

import jax
import jax.numpy as jnp
from jax import lax
from jax.experimental import pallas as pl
from jax.experimental.pallas import tpu as pltpu
from jax.sharding import PartitionSpec as P

MESH = pl.DeviceIdType.MESH
LANES = 128
CHUNKS = 8
F32, BF16 = jnp.float32, jnp.bfloat16


def rounded(value):
    return value.astype(BF16).astype(F32)


def dot(left, right, dims=((1,), (0,))):
    return lax.dot_general(left, right, (dims, ((), ())), preferred_element_type=F32)


def left_form(wide, dim):
    lane = lax.broadcasted_iota(jnp.int32, wide.shape, 1)
    norm = jnp.sum(jnp.where((lane >= dim) & (lane < dim + 3), wide, 0.0), axis=1, keepdims=True)
    left = jnp.where(lane < dim, 2.0 * wide, jnp.where(lane < dim + 3, -1.0, 0.0))
    return left.astype(BF16), norm


def reduce_bits(level):
    return [0] + list(range(level - 1, 0, -1)) if level else []


def plan(levels):
    names = []
    for level in range(levels):
        for bit in reduce_bits(level):
            names += [("rs", level, bit), ("ag", level, bit)]
        names += [("ex", level), ("pt", level)]
    for chunk in range(CHUNKS + 1):
        names += [("own_mate", chunk), ("own_x", chunk), ("fwd", chunk), ("fwd_mate", chunk)]
    return {name: at for at, name in enumerate(names)}


def body(
    count, slots,
    pts, w, interp, trans, mask, index,
    out,
    rown, lown, nown, rbuf, wbuf, near, lw, keep, tx, rx, sib, pbuf, psib, far,
    send_sem, recv_sem,
):
    me = lax.axis_index("leaf")
    core, chip = lax.rem(me, 2), lax.rem(me // 2, 2)
    dim, npts = pts.shape
    rank, rhs = lw.shape
    levels = trans.shape[0]
    deep = rown.shape[0]
    scale = math.log2(math.e) / dim

    def partner(bit):
        on = lax.rem(me // (1 << bit), 2)
        return me + (1 - 2 * on) * (1 << bit), on

    mate, xmate = partner(0)[0], partner(1)[0]
    ahead = me + 4 * (1 - 2 * chip)
    behind = me - 4 * (1 - 2 * chip)
    has_ahead = (ahead >= 0) & (ahead < count)
    has_behind = (behind >= 0) & (behind < count)

    def copy(name, src, dst, device):
        at = slots[name]
        return pltpu.make_async_remote_copy(
            src_ref=src, dst_ref=dst, send_sem=send_sem.at[at], recv_sem=recv_sem.at[at],
            device_id=(device,), device_id_type=MESH,
        )

    barrier = pltpu.get_barrier_semaphore()
    for bit in range(levels):
        pl.semaphore_signal(barrier, inc=1, device_id=(partner(bit)[0],), device_id_type=MESH)
    for other, there in ((ahead, has_ahead), (behind, has_behind)):
        @pl.when(there)
        def _():
            pl.semaphore_signal(barrier, inc=1, device_id=(other,), device_id_type=MESH)

    wide = pts[...].astype(F32)
    norm = jnp.sum(wide * wide, axis=0, keepdims=True)
    high = rounded(norm)
    middle = rounded(norm - high)
    low = norm - high - middle
    row = lax.broadcasted_iota(jnp.int32, (LANES - dim, npts), 0)
    extra = jnp.where(row == 0, high, jnp.where(row == 1, middle, jnp.where(row == 2, low, 0.0)))
    full = jnp.concatenate([wide, extra], axis=0)
    rown[...] = full[:deep].astype(BF16)
    left, norm_column = left_form(jnp.transpose(full), dim)
    lown[...] = left
    nown[...] = norm_column
    chosen = (lax.broadcasted_iota(jnp.int32, (npts, rank), 0) == index[...]).astype(BF16)
    pbuf[0] = jnp.transpose(dot(full.astype(BF16), chosen)).astype(BF16)

    pl.semaphore_wait(barrier, levels + has_ahead.astype(jnp.int32) + has_behind.astype(jnp.int32))

    step = npts // CHUNKS

    def part(chunk):
        return pl.ds((chunk - 1) * step, step)

    def own(kind, chunk, slot, device):
        if chunk == 0:
            return copy((kind, 0), rown, rbuf.at[slot], device)
        return copy((kind, chunk), w.at[part(chunk)], wbuf.at[slot, part(chunk)], device)

    def pass_on(kind, chunk, source, slot, device):
        if chunk == 0:
            return copy((kind, 0), rbuf.at[source], rbuf.at[slot], device)
        return copy((kind, chunk), wbuf.at[source, part(chunk)], wbuf.at[slot, part(chunk)], device)

    def points_copy(level):
        return copy(("pt", level), pbuf.at[level], psib.at[level], partner(level)[0])

    def points_next(level):
        points_copy(level).wait()
        if level + 1 == levels:
            return
        group, width = 1 << level, rank >> level

        def halved(ref):
            return ref[level].reshape(group, width, LANES)[:, : width // 2].reshape(rank // 2, LANES)

        mine, theirs = halved(pbuf), halved(psib)
        upper = partner(level)[1] == 1
        pbuf[level + 1, : rank // 2] = jnp.where(upper, theirs, mine)
        pbuf[level + 1, rank // 2 :] = jnp.where(upper, mine, theirs)
        points_copy(level + 1).start()

    points_copy(0).start()

    def send_x(*chunks):
        for chunk in chunks:
            own("own_x", chunk, 0, xmate).start()

    send_x(0, 1)

    lw[...] = dot(interp[...], w[...], ((0,), (0,))).astype(BF16)
    points_next(0)
    send_x(2)
    half = rank // 2
    kept_at = pl.multiple_of(core * half, half)
    sent_at = pl.multiple_of((1 - core) * half, half)

    def geometry(level, upto):
        bits = reduce_bits(level)
        offset, length = 0, rank
        for bit in bits[:upto]:
            length //= 2
            offset = offset + partner(bit)[1] * length
        if upto:
            offset = pl.multiple_of(offset, length)
        return offset, length

    def reduce_copy(level, at):
        bit = reduce_bits(level)[at]
        length = rank >> (at + 1)
        rows = pl.ds(rank - 2 * length, length)
        return copy(("rs", level, bit), tx.at[level, rows], rx.at[level, rows], partner(bit)[0])

    def exchange_copy(level):
        offset, length = geometry(level, level)
        rows = pl.ds(0 if level == 0 else rank - length, length)
        return copy(("ex", level), tx.at[level, rows], sib.at[level, pl.ds(offset, length)], partner(level)[0])

    def gather_copy(level, at):
        bit = reduce_bits(level)[at]
        offset, length = geometry(level, at + 1)
        rows = pl.ds(offset, length)
        return copy(("ag", level, bit), sib.at[level, rows], sib.at[level, rows], partner(bit)[0])

    for level in range(levels - 1, 0, -1):
        tx[level, :half] = dot(trans[level, :, pl.ds(sent_at, half)], lw[...], ((0,), (0,))).astype(BF16)
        reduce_copy(level, 0).start()
        keep[level] = dot(trans[level, :, pl.ds(kept_at, half)], lw[...], ((0,), (0,)))
    tx[0] = dot(trans[0], lw[...], ((0,), (0,))).astype(BF16)
    exchange_copy(0).start()
    for chunk in range(CHUNKS + 1):
        own("own_mate", chunk, 2, mate).start()

    def chain(level):
        bits = reduce_bits(level)
        for at, bit in enumerate(bits):
            reduce_copy(level, at).wait()
            length = rank >> (at + 1)
            total = keep[level, :length] + rx[level, pl.ds(rank - 2 * length, length)].astype(F32)
            if at + 1 < len(bits):
                shorter = length // 2
                upper = partner(bits[at + 1])[1] == 1
                first, second = total[:shorter], total[shorter:]
                tx[level, pl.ds(rank - length, shorter)] = jnp.where(upper, first, second).astype(BF16)
                reduce_copy(level, at + 1).start()
                keep[level, :shorter] = jnp.where(upper, second, first)
            else:
                tx[level, pl.ds(rank - length, length)] = total.astype(BF16)
                exchange_copy(level).start()
            yield
        exchange_copy(level).wait()
        for at in range(len(bits) - 1, -1, -1):
            gather_copy(level, at).start()
            yield
            gather_copy(level, at).wait()

    chains = [chain(level) for level in range(levels)]

    def advance(*which):
        for level in which:
            next(chains[level], None)

    even = chip == 0
    flags = [
        jnp.where(even, mask[0, 3], mask[0, 0]),
        jnp.where(even, mask[0, 0], mask[0, 3]),
        jnp.where(core == 0, mask[0, 2], mask[0, 1]),
        jnp.where(core == 0, mask[0, 1], mask[0, 2]),
    ]
    block = 256

    def near_part(right, weights, flag, first=0, last=npts // block):
        @pl.loop(first, last)
        def _(at):
            rows = pl.ds(pl.multiple_of(at * block, block), block)
            power = dot(lown[rows, :deep], right[...]) - nown[rows]
            tile = jnp.exp2(power * scale).astype(BF16)
            value = dot(tile, weights[...])
            near[rows] = value if flag is None else near[rows] + flag.astype(F32) * value

    def near_slot(slot):
        near_part(rbuf.at[slot], wbuf.at[slot], flags[slot])

    def couple(level):
        left, norm_own = left_form(pbuf[level].astype(F32), dim)
        power = dot(left, psib[level], ((1,), (1,))) - norm_own
        tile = jnp.exp2(power * scale).astype(BF16)
        coupled = dot(tile, sib[level]).astype(BF16)
        term = dot(trans[level], coupled)
        far[...] = term if level == 0 else far[...] + term

    direct = core == chip

    def relay(*chunks):
        for chunk in chunks:
            own("own_x", chunk, 0, xmate).wait_recv()

            @pl.when(has_ahead)
            def _():
                pass_on("fwd", chunk, 0, 1, ahead).start()

            @pl.when(direct)
            def _():
                pass_on("fwd_mate", chunk, 0, 3, mate).start()

    def relay_on(*chunks):
        for chunk in chunks:
            @pl.when(has_behind)
            def _():
                pass_on("fwd", chunk, 0, 1, ahead).wait_recv()

                @pl.when(jnp.logical_not(direct))
                def _():
                    pass_on("fwd_mate", chunk, 1, 3, mate).start()

    tiles = npts // block
    advance(4, 3, 2, 1)
    send_x(3)
    near_part(rown, w, None, 0, tiles // 2)
    relay(0, 1)
    points_next(1)

    advance(4, 3, 2)
    send_x(4)
    near_part(rown, w, None, tiles // 2, tiles)
    relay(2)
    points_next(2)

    advance(4, 3, 2)
    send_x(5)
    for chunk in range(CHUNKS + 1):
        own("own_mate", chunk, 2, mate).wait_recv()
    near_slot(2)
    relay(3)
    relay_on(0, 1)
    points_next(3)

    advance(4, 3, 2)
    send_x(6)
    advance(1, 0)
    couple(0)
    relay(4)
    relay_on(2)
    points_next(4)

    advance(4, 3, 2)
    send_x(7)
    advance(1)
    couple(1)
    relay(5)
    relay_on(3)

    advance(4, 3)
    send_x(8)
    couple(2)
    relay(6)
    relay_on(4)

    advance(4, 3)
    couple(3)
    relay(7)
    relay_on(5)

    advance(4)
    relay(8)
    near_slot(0)
    relay_on(6)

    advance(4)
    couple(4)
    relay_on(7, 8)

    @pl.when(has_behind)
    def _():
        near_slot(1)

    @pl.when(has_behind | jnp.logical_not(direct))
    def _():
        for chunk in range(CHUNKS + 1):
            pass_on("fwd_mate", chunk, 0, 3, mate).wait_recv()
        near_slot(3)

    total = far[...].astype(BF16)

    @pl.loop(0, npts // block)
    def _(at):
        rows = pl.ds(pl.multiple_of(at * block, block), block)
        out[rows] = (near[rows] + dot(interp[rows], total)).astype(out.dtype)

    for chunk in range(CHUNKS + 1):
        own("own_mate", chunk, 2, mate).wait_send()
        own("own_x", chunk, 0, xmate).wait_send()

        @pl.when(has_ahead)
        def _():
            pass_on("fwd", chunk, 0, 1, ahead).wait_send()

        @pl.when(has_behind | direct)
        def _():
            pass_on("fwd_mate", chunk, 0, 3, mate).wait_send()


def per_device(points, weights, interp, transfers, near_mask, skel_index):
    count = lax.axis_size("leaf")
    dim, npts = points.shape
    rhs, rank = weights.shape[1], interp.shape[1]
    levels = transfers.shape[1]
    deep = -(-(dim + 3) // 16) * 16
    slots = plan(levels)
    vmem = pl.BlockSpec(memory_space=pltpu.VMEM)
    return pl.pallas_call(
        functools.partial(body, count, slots),
        out_shape=jax.ShapeDtypeStruct((npts, rhs), BF16),
        in_specs=[vmem] * 4 + [pl.BlockSpec(memory_space=pltpu.SMEM), vmem],
        out_specs=vmem,
        scratch_shapes=[
            pltpu.VMEM((deep, npts), BF16),
            pltpu.VMEM((npts, LANES), BF16),
            pltpu.VMEM((npts, 1), F32),
            pltpu.VMEM((4, deep, npts), BF16),
            pltpu.VMEM((4, npts, rhs), BF16),
            pltpu.VMEM((npts, rhs), F32),
            pltpu.VMEM((rank, rhs), BF16),
            pltpu.VMEM((levels, rank // 2, rhs), F32),
            pltpu.VMEM((levels, rank, rhs), BF16),
            pltpu.VMEM((levels, rank, rhs), BF16),
            pltpu.VMEM((levels, rank, rhs), BF16),
            pltpu.VMEM((levels, rank, LANES), BF16),
            pltpu.VMEM((levels, rank, LANES), BF16),
            pltpu.VMEM((rank, rhs), F32),
            pltpu.SemaphoreType.DMA((len(slots),)),
            pltpu.SemaphoreType.DMA((len(slots),)),
        ],
        compiler_params=pltpu.CompilerParams(
            collective_id=0, has_side_effects=True, vmem_limit_bytes=60 * 2**20
        ),
    )(points, weights, interp, transfers[0], near_mask, skel_index)


def solution(mesh):
    return jax.shard_map(
        per_device,
        mesh=mesh,
        in_specs=(
            P(None, "leaf"),
            P("leaf", None),
            P("leaf", None),
            P("leaf", None, None, None),
            P("leaf", None),
            P("leaf", None),
        ),
        out_specs=P("leaf", None),
        check_vma=False,
    )
```

profile of v0, /device:TPU:12, one launch (start us, length us, event | category | flops | bytes accessed | tf_op | source)
XLA Modules:
  0.0 75.4 jit_solution(18004400787106119403)
XLA Ops:
  0.0 73.1 %shard_map.64 = bf16[1024,512]{1,0:T(8,128)(2,1)} custom-call(bf16[64,1024]{1,0:T(8,128)(2,1)} %pts.1, bf16[1024,512]{1,0:T(8,128)(2,1)} %w.1, bf16[1024,512]{1,0:T(8,128)(2,1)} %interp.1, bf16[5,512,512]{2,1,0:T(8,128)(2,1)} %bitcast.1, s32[1,4]{1,0:T(1,128)} %mask.1, s32[1,512]{1,0:T(1,128)} %index.1), custom_call_target="tpu_custom_call" | custom-call | tf_op jit(solution)/shard_map/pallas_call | solution.py:365
  73.2 2.3 %copy.8 = bf16[1024,512]{1,0:T(8,128)(2,1)} copy(bf16[1024,512]{1,0:T(8,128)(2,1)} %shard_map.64) | data formatting | bytes 2097152
where the time goes:
time: 75.6 us; the launch traced here: 75.4 us
  Pallas kernels  73.1 us (97%)
  local copies, waits for them, and re-layouts  2.26 us (3%)
    pallas_call x1, Pallas kernels, per_device(): pl.pallas_call(functools.partial(body, count, slots), out_shape=jax.Shape...  73.1 us
    unnamed x1, local copies, waits for them, and re-layouts  2.26 us

commit v1 on v0

v1 whole, which is shorter than its diff:
```python
import functools
import math

import jax
import jax.numpy as jnp
from jax import lax
from jax.experimental import pallas as pl
from jax.experimental.pallas import tpu as pltpu
from jax.sharding import PartitionSpec as P

MESH = pl.DeviceIdType.MESH
LANES = 128
CHUNKS = 8
LAG = 3
F32, BF16 = jnp.float32, jnp.bfloat16


def rounded(value):
    return value.astype(BF16).astype(F32)


def dot(left, right, dims=((1,), (0,))):
    return lax.dot_general(left, right, (dims, ((), ())), preferred_element_type=F32)


def left_form(wide, dim):
    lane = lax.broadcasted_iota(jnp.int32, wide.shape, 1)
    norm = jnp.sum(jnp.where((lane >= dim) & (lane < dim + 3), wide, 0.0), axis=1, keepdims=True)
    left = jnp.where(lane < dim, 2.0 * wide, jnp.where(lane < dim + 3, -1.0, 0.0))
    return left.astype(BF16), norm


def reduce_bits(level):
    return list(range(level - 1, 0, -1))


def plan(levels):
    names = []
    for level in range(levels):
        for bit in reduce_bits(level):
            names += [("rs", level, bit), ("ag", level, bit)]
        names += [("rs0", level), ("ag0", level), ("ex", level), ("pt", level), ("pt0", level)]
    names += [("own", 0), ("own", 1)]
    for chunk in range(CHUNKS + 1):
        for leaf in range(2):
            names += [("bx", leaf, chunk), ("fw", leaf, chunk)]
        names += [("bm", slot, chunk) for slot in range(4)]
    return {name: at for at, name in enumerate(names)}


def body(
    count, slots,
    pts, w, interp, trans, mask, index,
    out,
    rown, lown, nown, rbuf, wbuf, near, lw, keep, tx, rx, mx, sib, pbuf, psib, far,
    send_sem, recv_sem,
):
    me = lax.axis_index("leaf")
    core, chip = lax.rem(me, 2), lax.rem(me // 2, 2)
    even = chip == 0
    dim, npts = pts.shape
    rank, rhs = lw.shape
    half = rank // 2
    levels = trans.shape[0]
    deep = rown.shape[0]
    scale = math.log2(math.e) / dim

    def partner(bit):
        on = lax.rem(me // (1 << bit), 2)
        return me + (1 - 2 * on) * (1 << bit), on

    mate, xmate = partner(0)[0], partner(1)[0]
    ahead = me + 4 * (1 - 2 * chip)
    behind = me - 4 * (1 - 2 * chip)
    has_ahead = (ahead >= 0) & (ahead < count)
    has_behind = (behind >= 0) & (behind < count)

    def copy(name, src, dst, device):
        at = slots[name]
        return pltpu.make_async_remote_copy(
            src_ref=src, dst_ref=dst, send_sem=send_sem.at[at], recv_sem=recv_sem.at[at],
            device_id=(device,), device_id_type=MESH,
        )

    barrier = pltpu.get_barrier_semaphore()
    for bit in range(levels):
        pl.semaphore_signal(barrier, inc=1, device_id=(partner(bit)[0],), device_id_type=MESH)
    for other, there in ((ahead, has_ahead), (behind, has_behind)):
        @pl.when(there)
        def _():
            pl.semaphore_signal(barrier, inc=1, device_id=(other,), device_id_type=MESH)

    wide = pts[...].astype(F32)
    norm = jnp.sum(wide * wide, axis=0, keepdims=True)
    high = rounded(norm)
    middle = rounded(norm - high)
    low = norm - high - middle
    row = lax.broadcasted_iota(jnp.int32, (LANES - dim, npts), 0)
    extra = jnp.where(row == 0, high, jnp.where(row == 1, middle, jnp.where(row == 2, low, 0.0)))
    full = jnp.concatenate([wide, extra], axis=0)
    rown[...] = full[:deep].astype(BF16)

    pl.semaphore_wait(barrier, levels + has_ahead.astype(jnp.int32) + has_behind.astype(jnp.int32))

    step = npts // CHUNKS

    def part(chunk):
        return pl.ds((chunk - 1) * step, step)

    def own(which):
        if which == 0:
            return copy(("own", 0), rown, rbuf.at[4], mate)
        return copy(("own", 1), w, wbuf.at[4], mate)

    def between(name, src, dst, chunk, device):
        if chunk == 0:
            return copy(name, src[0], dst[0], device)
        return copy(name, src[1].at[part(chunk)], dst[1].at[part(chunk)], device)

    def leaf_slot(slot):
        return rbuf.at[slot], wbuf.at[slot]

    def to_x(leaf, chunk):
        source = (rown, w) if leaf == 0 else leaf_slot(4)
        return between(("bx", leaf, chunk), source, leaf_slot(leaf), chunk, xmate)

    def forward(leaf, chunk):
        return between(("fw", leaf, chunk), leaf_slot(leaf), leaf_slot(2 + leaf), chunk, ahead)

    def to_mate(slot, chunk):
        return between(("bm", slot, chunk), leaf_slot(slot), leaf_slot(slot), chunk, mate)

    chunks = range(CHUNKS + 1)

    own(1).start()
    own(0).start()

    @pl.when(core == 0)
    def _():
        for chunk in chunks:
            to_x(0, chunk).start()

    left, norm_column = left_form(jnp.transpose(full), dim)
    lown[...] = left
    nown[...] = norm_column
    chosen = (lax.broadcasted_iota(jnp.int32, (npts, rank), 0) == index[...]).astype(BF16)
    pbuf[0] = jnp.transpose(dot(full.astype(BF16), chosen)).astype(BF16)

    def points_copy(level):
        return copy(("pt", level), pbuf.at[level], psib.at[level], partner(level)[0])

    def points_mate(level):
        return copy(("pt0", level), psib.at[level], psib.at[level], mate)

    def points_join(level):
        if level + 1 == levels:
            return
        group, width = 1 << level, rank >> level

        def halved(ref):
            return ref[level].reshape(group, width, LANES)[:, : width // 2].reshape(rank // 2, LANES)

        mine, theirs = halved(pbuf), halved(psib)
        upper = partner(level)[1] == 1
        pbuf[level + 1, : rank // 2] = jnp.where(upper, theirs, mine)
        pbuf[level + 1, rank // 2 :] = jnp.where(upper, mine, theirs)

    points_copy(0).start()

    lw[...] = dot(interp[...], w[...], ((0,), (0,))).astype(BF16)
    kept_at = pl.multiple_of(core * half, half)
    sent_at = pl.multiple_of((1 - core) * half, half)

    def geometry(level, upto):
        bits = reduce_bits(level)
        offset, length = 0, rank
        for bit in bits[:upto]:
            length //= 2
            offset = offset + partner(bit)[1] * length
        if upto:
            offset = pl.multiple_of(offset, length)
        return offset, length

    def term_copy(level):
        if level == 1:
            return copy(("rs0", 1), tx.at[1, pl.ds(0, half)], mx.at[1, pl.ds(0, half)], mate)
        return copy(("rs0", level), tx.at[level], mx.at[level], mate)

    def reduce_copy(level, at):
        bit = reduce_bits(level)[at]
        length = rank >> (at + 1)
        rows = pl.ds(rank - 2 * length, length)
        return copy(("rs", level, bit), tx.at[level, rows], rx.at[level, rows], partner(bit)[0])

    def exchange_copy(level):
        if level == 0:
            return copy(("ex", 0), tx.at[0], sib.at[0], mate)
        if level == 1:
            return copy(("ex", 1), tx.at[1, pl.ds(half, half)], sib.at[1, pl.ds(kept_at, half)], xmate)
        offset, length = geometry(level, level - 1)
        rows = pl.ds(rank - length, length)
        return copy(("ex", level), tx.at[level, rows], sib.at[level, pl.ds(offset, length)], partner(level)[0])

    def gather_copy(level, at):
        bit = reduce_bits(level)[at]
        offset, length = geometry(level, at + 1)
        rows = pl.ds(offset, length)
        return copy(("ag", level, bit), sib.at[level, rows], sib.at[level, rows], partner(bit)[0])

    def share_copy(level):
        if level == 1:
            rows = pl.ds(kept_at, half)
            return copy(("ag0", 1), sib.at[1, rows], sib.at[1, rows], mate)
        return copy(("ag0", level), sib.at[level], sib.at[level], mate)

    def term(level, rows=None):
        block = trans[level] if rows is None else trans[level, :, rows]
        return dot(block, lw[...], ((0,), (0,)))

    block = 256
    tiles = npts // block

    def near_part(right, weights, flag, first=0, last=tiles):
        @pl.loop(first, last)
        def _(at):
            rows = pl.ds(pl.multiple_of(at * block, block), block)
            power = dot(lown[rows, :deep], right[...]) - nown[rows]
            tile = jnp.exp2(power * scale).astype(BF16)
            value = dot(tile, weights[...])
            near[rows] = value if flag is None else near[rows] + flag.astype(F32) * value

    def near_self(first, last):
        near_part(rown, w, None, first, last)

    def near_slot(slot, flag, first=0, last=tiles):
        near_part(rbuf.at[slot], wbuf.at[slot], flag, first, last)

    def couple(level):
        left, norm_own = left_form(pbuf[level].astype(F32), dim)
        power = dot(left, psib[level], ((1,), (1,))) - norm_own
        tile = jnp.exp2(power * scale).astype(BF16)
        coupled = dot(tile, sib[level]).astype(BF16)
        value = dot(trans[level], coupled)
        far[...] = value if level == 0 else far[...] + value

    def level_one_ready():
        term_copy(1).wait_recv()
        tx[1, half:] = (keep[1, :half] + mx[1, :half].astype(F32)).astype(BF16)

    def level_zero_and_one():
        tx[1, :half] = term(1, pl.ds(sent_at, half)).astype(BF16)
        term_copy(1).start()
        keep[1, :half] = term(1, pl.ds(kept_at, half))
        tx[0] = term(0).astype(BF16)
        exchange_copy(0).start()

    @pl.when(core == 0)
    def _():
        for level in range(levels - 1, 1, -1):
            tx[level] = term(level).astype(BF16)
            term_copy(level).start()
        own(1).wait_recv()
        own(0).wait_recv()
        for chunk in chunks:
            to_x(1, chunk).start()
        level_zero_and_one()
        level_one_ready()
        exchange_copy(1).start()
        points_copy(0).wait()
        points_join(0)

        flags = [
            jnp.where(even, mask[0, 3], mask[0, 0]),
            jnp.where(even, mask[0, 0], mask[0, 3]),
            mask[0, 1],
        ]
        third = jnp.where(even, 3, 1)

        def relay(at):
            leaf, chunk = divmod(at, CHUNKS + 1)
            to_x(leaf, chunk).wait_recv()

            @pl.when(has_ahead)
            def _():
                forward(leaf, chunk).start()

            if leaf == 1:
                to_mate(1, chunk).start()
            else:
                @pl.when(even)
                def _():
                    to_mate(0, chunk).start()

        def collect(at):
            leaf, chunk = divmod(at, CHUNKS + 1)

            @pl.when(has_behind)
            def _():
                forward(leaf, chunk).wait_recv()
                if leaf == 1:
                    to_mate(3, chunk).start()

            if leaf == 0:
                @pl.when(has_behind & jnp.logical_not(even))
                def _():
                    to_mate(2, chunk).start()

        def points_here(level):
            points_mate(level).wait_recv()
            points_join(level)

        def far_level(level):
            share_copy(level).wait_recv()
            couple(level)

        def level_zero():
            exchange_copy(0).wait_recv()
            couple(0)

        def slot_two(first, last):
            @pl.when(has_behind)
            def _():
                near_slot(2, flags[1], first, last)

        def two():
            points_here(1)
            points_here(2)
            far_level(2)

        work = {}
        for at in range(4):
            work[at] = functools.partial(near_self, at, at + 1)
            work[4 + at] = functools.partial(near_slot, 4, mask[0, 2], at, at + 1)
            work[10 + at] = functools.partial(near_slot, 0, flags[0], at, at + 1)
        work[8] = level_zero
        work[14] = functools.partial(slot_two, 0, 2)
        work[15] = functools.partial(slot_two, 2, 4)
        work[16] = two

        total = 2 * (CHUNKS + 1)
        for at in range(total + LAG):
            if at < total:
                relay(at)
            if at >= LAG:
                collect(at - LAG)
            if at in work:
                work[at]()
        points_here(3)
        far_level(3)
        points_here(4)
        far_level(4)

        @pl.when(has_behind | jnp.logical_not(even))
        def _():
            near_slot(third, flags[2])

        exchange_copy(1).wait_recv()
        share_copy(1).start()
        far_level(1)

    @pl.when(core == 1)
    def _():
        def chain(level):
            bits = reduce_bits(level)
            term_copy(level).wait_recv()
            offset, length = 0, rank

            def incoming(at, start):
                if at == 0:
                    return mx[level, pl.ds(start, length // 2)].astype(F32)
                return rx[level, pl.ds(pl.multiple_of(rank - 2 * length + start, length // 2), length // 2)].astype(F32)

            for at, bit in enumerate(bits):
                shorter = length // 2
                on = partner(bit)[1]
                sent = pl.multiple_of((1 - on) * shorter, shorter)
                kept = pl.multiple_of(on * shorter, shorter)
                there = pl.ds(pl.multiple_of(offset + sent, shorter), shorter)
                here = pl.ds(pl.multiple_of(offset + kept, shorter), shorter)
                tx[level, rank - length : rank - length + shorter] = (
                    keep[level, there] + incoming(at, sent)
                ).astype(BF16)
                reduce_copy(level, at).start()
                keep[level, here] = keep[level, here] + incoming(at, kept)
                offset, length = offset + kept, shorter
                yield
                reduce_copy(level, at).wait()
            last = rx[level, rank - 2 * length : rank - length].astype(F32)
            tx[level, rank - length :] = (
                keep[level, pl.ds(pl.multiple_of(offset, length), length)] + last
            ).astype(BF16)
            exchange_copy(level).start()
            yield
            exchange_copy(level).wait()
            for at in range(len(bits) - 1, -1, -1):
                gather_copy(level, at).start()
                yield
                gather_copy(level, at).wait()
            share_copy(level).start()

        chains = {level: chain(level) for level in range(2, levels)}

        def advance(*which):
            for level in which:
                next(chains[level], None)

        def points_on(level):
            points_copy(level).wait()
            if level:
                points_mate(level).start()
            points_join(level)
            if level + 1 < levels:
                points_copy(level + 1).start()

        keep[4] = term(4)
        keep[3] = term(3)
        advance(4)
        keep[2] = term(2)
        advance(3)
        level_zero_and_one()
        advance(2)
        points_on(0)
        near_self(0, 2)
        advance(4, 3)
        own(1).wait_recv()
        own(0).wait_recv()
        near_self(2, 4)
        advance(2)
        advance(4, 3)
        level_one_ready()
        points_on(1)
        near_slot(4, mask[0, 1], 0, 2)
        advance(4, 3)
        near_slot(4, mask[0, 1], 2, 4)
        points_on(2)
        advance(4, 2)
        exchange_copy(1).start()
        advance(3, 4)
        points_on(3)
        exchange_copy(0).wait_recv()
        couple(0)
        advance(4, 3, 2)
        couple(2)
        couple(3)
        points_on(4)

        flags = [
            mask[0, 2],
            jnp.where(even, mask[0, 3], mask[0, 0]),
            jnp.where(even, mask[0, 0], mask[0, 3]),
        ]

        @pl.when(even)
        def _():
            for chunk in chunks:
                to_mate(0, chunk).wait_recv()

        @pl.when(has_behind & jnp.logical_not(even))
        def _():
            for chunk in chunks:
                to_mate(2, chunk).wait_recv()

        @pl.when(has_behind | even)
        def _():
            near_slot(jnp.where(even, 0, 2), flags[0])

        for chunk in chunks:
            to_mate(1, chunk).wait_recv()
        near_slot(1, flags[1])
        advance(4)
        couple(4)

        @pl.when(has_behind)
        def _():
            for chunk in chunks:
                to_mate(3, chunk).wait_recv()
            near_slot(3, flags[2])

        exchange_copy(1).wait_recv()
        share_copy(1).start()
        share_copy(1).wait_recv()
        couple(1)

    total = far[...].astype(BF16)

    @pl.loop(0, tiles)
    def _(at):
        rows = pl.ds(pl.multiple_of(at * block, block), block)
        out[rows] = (near[rows] + dot(interp[rows], total)).astype(out.dtype)

    own(0).wait_send()
    own(1).wait_send()
    term_copy(1).wait_send()
    exchange_copy(0).wait_send()
    exchange_copy(1).wait_send()
    share_copy(1).wait_send()

    @pl.when(core == 0)
    def _():
        for level in range(2, levels):
            term_copy(level).wait_send()
        for chunk in chunks:
            to_x(0, chunk).wait_send()
            to_x(1, chunk).wait_send()

            @pl.when(has_ahead)
            def _():
                forward(0, chunk).wait_send()
                forward(1, chunk).wait_send()

            to_mate(1, chunk).wait_send()

            @pl.when(even)
            def _():
                to_mate(0, chunk).wait_send()

            @pl.when(has_behind)
            def _():
                to_mate(3, chunk).wait_send()

            @pl.when(has_behind & jnp.logical_not(even))
            def _():
                to_mate(2, chunk).wait_send()

    @pl.when(core == 1)
    def _():
        for level in range(2, levels):
            share_copy(level).wait_send()
        for level in range(1, levels):
            points_mate(level).wait_send()


def per_device(points, weights, interp, transfers, near_mask, skel_index):
    count = lax.axis_size("leaf")
    dim, npts = points.shape
    rhs, rank = weights.shape[1], interp.shape[1]
    levels = transfers.shape[1]
    deep = -(-(dim + 3) // 16) * 16
    slots = plan(levels)
    vmem = pl.BlockSpec(memory_space=pltpu.VMEM)
    return pl.pallas_call(
        functools.partial(body, count, slots),
        out_shape=jax.ShapeDtypeStruct((npts, rhs), BF16),
        in_specs=[vmem] * 4 + [pl.BlockSpec(memory_space=pltpu.SMEM), vmem],
        out_specs=vmem,
        scratch_shapes=[
            pltpu.VMEM((deep, npts), BF16),
            pltpu.VMEM((npts, LANES), BF16),
            pltpu.VMEM((npts, 1), F32),
            pltpu.VMEM((5, deep, npts), BF16),
            pltpu.VMEM((5, npts, rhs), BF16),
            pltpu.VMEM((npts, rhs), F32),
            pltpu.VMEM((rank, rhs), BF16),
            pltpu.VMEM((levels, rank, rhs), F32),
            pltpu.VMEM((levels, rank, rhs), BF16),
            pltpu.VMEM((levels, rank, rhs), BF16),
            pltpu.VMEM((levels, rank, rhs), BF16),
            pltpu.VMEM((levels, rank, rhs), BF16),
            pltpu.VMEM((levels, rank, LANES), BF16),
            pltpu.VMEM((levels, rank, LANES), BF16),
            pltpu.VMEM((rank, rhs), F32),
            pltpu.SemaphoreType.DMA((len(slots),)),
            pltpu.SemaphoreType.DMA((len(slots),)),
        ],
        compiler_params=pltpu.CompilerParams(
            collective_id=0, has_side_effects=True, vmem_limit_bytes=60 * 2**20
        ),
    )(points, weights, interp, transfers[0], near_mask, skel_index)


def solution(mesh):
    return jax.shard_map(
        per_device,
        mesh=mesh,
        in_specs=(
            P(None, "leaf"),
            P("leaf", None),
            P("leaf", None),
            P("leaf", None, None, None),
            P("leaf", None),
            P("leaf", None),
        ),
        out_specs=P("leaf", None),
        check_vma=False,
    )
```

time: 75.6 us -> 72.2 us (0.955)
  the two profiles are of different devices: /device:TPU:12 before, /device:TPU:7 now
where the time goes in v1:
time: 72.2 us; the launch traced here: 72.1 us
  Pallas kernels  69.8 us (97%)
  local copies, waits for them, and re-layouts  2.26 us (3%)
    pallas_call x1, Pallas kernels, per_device(): pl.pallas_call(functools.partial(body, count, slots), out_shape=jax.Shape...  69.8 us
    unnamed x1, local copies, waits for them, and re-layouts  2.26 us

profile of v1, /device:TPU:7, one launch (start us, length us, event | category | flops | bytes accessed | tf_op | source)
XLA Modules:
  0.0 72.1 jit_solution(16068416451750613202)
XLA Ops:
  0.0 69.8 %shard_map.64 = bf16[1024,512]{1,0:T(8,128)(2,1)} custom-call(bf16[64,1024]{1,0:T(8,128)(2,1)} %pts.1, bf16[1024,512]{1,0:T(8,128)(2,1)} %w.1, bf16[1024,512]{1,0:T(8,128)(2,1)} %interp.1, bf16[5,512,512]{2,1,0:T(8,128)(2,1)} %bitcast.1, s32[1,4]{1,0:T(1,128)} %mask.1, s32[1,512]{1,0:T(1,128)} %index.1), custom_call_target="tpu_custom_call" | custom-call | tf_op jit(solution)/shard_map/pallas_call | solution.py:541
  69.8 2.3 %copy.8 = bf16[1024,512]{1,0:T(8,128)(2,1)} copy(bf16[1024,512]{1,0:T(8,128)(2,1)} %shard_map.64) | data formatting | bytes 2097152
